TPU v7x, 32 devices: a whole 2x2x4 slice. The times are simulated.
32 devices in a mesh: face: 8 (over z, x), band: 4 (over y, core).
Axes of the slice: x: 2, y: 2, z: 4, core: 2. Of those that a mesh axis runs over, the one named last changes fastest.
Arguments:
- node_latents: bfloat16 [8192, 512], P(('face', 'band')), may hold values from -6 to 6
- coarse_latents: bfloat16 [1024, 512], replicated, may hold values from -6 to 6
- edge_latents: bfloat16 [32768, 512], P(('face', 'band')), may hold values from -6 to 6
- up_latents: bfloat16 [8192, 512], P(('face', 'band')), may hold values from -6 to 6
- edge_weight_in: bfloat16 [1536, 512], replicated, may hold values from -0.15625 to 0.15625
- edge_weight_out: bfloat16 [512, 512], replicated, may hold values from -0.25 to 0.25
- edge_gain: float32 [512], replicated, may hold values from 0.5 to 1.5
- node_weight_in: bfloat16 [1024, 512], replicated, may hold values from -0.1875 to 0.1875
- node_weight_out: bfloat16 [512, 512], replicated, may hold values from -0.25 to 0.25
- node_gain: float32 [512], replicated, may hold values from 0.5 to 1.5
- nodes_cotangent: bfloat16 [8192, 512], P(('face', 'band')), may hold values from -6 to 6
- coarse_cotangent: bfloat16 [1024, 512], replicated, may hold values from -6 to 6
- edges_cotangent: bfloat16 [32768, 512], P(('face', 'band')), may hold values from -6 to 6
- ups_cotangent: bfloat16 [8192, 512], P(('face', 'band')), may hold values from -6 to 6
- send_rows: int32 [32, 32, 4], P(('face', 'band')), may hold values from 0 to 255, as said below
- edge_sender: int32 [32768], P(('face', 'band')), may hold values from 0 to 1407, as said below
- edge_receiver: int32 [32768], P(('face', 'band')), may hold values from 0 to 255
- up_sender: int32 [8192], P(('face', 'band')), may hold values from 0 to 255
- up_receiver: int32 [8192], P(('face', 'band')), may hold values from 0 to 1023
Outputs:
- grad_nodes: float32 [8192, 512], P(('face', 'band'))
- grad_coarse: float32 [1024, 512], replicated
- grad_edges: float32 [32768, 512], P(('face', 'band'))
- grad_ups: float32 [8192, 512], P(('face', 'band'))
- grad_edge_in: float32 [1536, 512], replicated
- grad_edge_out: float32 [512, 512], replicated
- grad_edge_gain: float32 [512], replicated
- grad_node_in: float32 [1024, 512], replicated
- grad_node_out: float32 [512, 512], replicated
- grad_node_gain: float32 [512], replicated
Inputs may be any that keep to these rules, and one draw needn't show every extreme that they name: `send_rows`: entry [s, p, k] is a row of device s's nodes sent to device p in slot k. Each pair uses its first few slots, at most 4; every device fills all 4 slots to at least one device, and in every draw some device receives 4 rows from every device. Unused slots hold 0 and no edge reads them. `edge_sender`: an edge of device p reads row t of p's sender table: its own node t below 256; slot k of the rows that device s sends to p for t = 256 + s * 4 + k, always a used slot; coarse node t - 384 from 384 on.
All inputs are finite; a program needn't handle non-finite values.
Results may differ from a plain program's by a relative error of at most 0.0068.
Values may be sent and summed in bfloat16 or wider, within the bound.
No kernel may reach another device: no remote copies, remote signals or barrier semaphores. Data moves between devices by JAX's collectives and lax.ppermute only.
A program may use at most 192 MiB of HBM per device.

v0:
```python
import math

import jax
import jax.numpy as jnp
from jax import lax
from jax.sharding import PartitionSpec as P

EPSILON = 1e-05


def mlp_forward(inputs, residual_base, first_weight, second_weight, gain_vec):
    pre_act = jnp.dot(inputs, first_weight, preferred_element_type=jnp.float32)
    hidden_act = jax.nn.silu(pre_act).astype(jnp.bfloat16)
    projected = jnp.dot(hidden_act, second_weight, preferred_element_type=jnp.float32)
    center = projected - jnp.mean(projected, axis=1, keepdims=True)
    inv_std = lax.rsqrt(jnp.mean(center * center, axis=1, keepdims=True) + EPSILON)
    normed = center * inv_std
    return (residual_base + normed * gain_vec, (pre_act, hidden_act, normed, inv_std))


def mlp_backward(inputs, first_weight, second_weight, gain_vec, cache_vals, cotangent):
    pre_act, hidden_act, normed, inv_std = cache_vals
    grad_gain = jnp.sum(cotangent * normed, axis=0)
    scaled = cotangent * gain_vec
    grad_proj = inv_std * (
        scaled
        - jnp.mean(scaled, axis=1, keepdims=True)
        - normed * jnp.mean(scaled * normed, axis=1, keepdims=True)
    )
    grad_proj = grad_proj.astype(jnp.bfloat16)
    grad_second = jnp.dot(hidden_act.T, grad_proj, preferred_element_type=jnp.float32)
    grad_hidden = jnp.dot(grad_proj, second_weight.T, preferred_element_type=jnp.float32)
    logistic = jax.nn.sigmoid(pre_act)
    grad_pre = (grad_hidden * logistic * (1.0 + pre_act * (1.0 - logistic))).astype(jnp.bfloat16)
    grad_first = jnp.dot(inputs.T, grad_pre, preferred_element_type=jnp.float32)
    grad_inputs = jnp.dot(grad_pre, first_weight.T, preferred_element_type=jnp.float32)
    return (grad_inputs, grad_first, grad_second, grad_gain)


def per_device(
    node_latents,
    coarse_latents,
    edge_latents,
    up_latents,
    edge_weight_in,
    edge_weight_out,
    edge_gain,
    node_weight_in,
    node_weight_out,
    node_gain,
    nodes_cotangent,
    coarse_cotangent,
    edges_cotangent,
    ups_cotangent,
    send_rows,
    edge_sender,
    edge_receiver,
    up_sender,
    up_receiver,
):
    latent_width = node_latents.shape[1]
    node_count = node_latents.shape[0]
    coarse_count = coarse_latents.shape[0]
    devices = lax.axis_size(("face", "band"))
    slot_count = send_rows.shape[2]
    import_count = devices * slot_count
    send_table = send_rows[0]
    outgoing = jnp.take(node_latents, send_table, axis=0)
    face_count = lax.axis_size("face")
    sectioned = outgoing.reshape(face_count, devices // face_count, slot_count, latent_width)
    incoming = lax.all_to_all(
        lax.all_to_all(sectioned, "face", split_axis=0, concat_axis=0, tiled=True),
        "band",
        split_axis=1,
        concat_axis=1,
        tiled=True,
    )
    sender_table = jnp.concatenate(
        [node_latents, incoming.reshape(import_count, latent_width), coarse_latents], 0
    )
    edge_inputs = jnp.concatenate(
        [
            edge_latents,
            jnp.take(sender_table, edge_sender, axis=0),
            jnp.take(node_latents, edge_receiver, axis=0),
        ],
        1,
    )
    edge_output, edge_cache = mlp_forward(
        edge_inputs, edge_latents.astype(jnp.float32), edge_weight_in, edge_weight_out, edge_gain
    )
    new_edges = edge_output.astype(jnp.bfloat16)
    receiver_onehot = (
        jnp.arange(node_count, dtype=jnp.int32)[:, None] == edge_receiver[None, :]
    ).astype(jnp.bfloat16)
    fine_total = jnp.dot(receiver_onehot, new_edges, preferred_element_type=jnp.float32)
    up_inputs = jnp.concatenate(
        [
            up_latents,
            jnp.take(node_latents, up_sender, axis=0),
            jnp.take(coarse_latents, up_receiver, axis=0),
        ],
        1,
    )
    up_output, up_cache = mlp_forward(
        up_inputs, up_latents.astype(jnp.float32), edge_weight_in, edge_weight_out, edge_gain
    )
    new_ups = up_output.astype(jnp.bfloat16)
    node_inputs = jnp.concatenate([node_latents, fine_total.astype(jnp.bfloat16)], 1)
    unused_node, node_cache = mlp_forward(
        node_inputs, node_latents.astype(jnp.float32), node_weight_in, node_weight_out, node_gain
    )
    node_grad_inputs, node_first, node_second, node_gain_grad = mlp_backward(
        node_inputs,
        node_weight_in,
        node_weight_out,
        node_gain,
        node_cache,
        nodes_cotangent.astype(jnp.float32),
    )
    row_ids = jnp.arange(coarse_count, dtype=jnp.int32)
    onehot_rows = (row_ids[:, None] == up_receiver[None, :]).astype(jnp.bfloat16)
    coarse_total = lax.psum(
        jnp.dot(onehot_rows, new_ups, preferred_element_type=jnp.float32), ("face", "band")
    )
    coarse_inputs = jnp.concatenate([coarse_latents, coarse_total.astype(jnp.bfloat16)], 1)
    unused_coarse, coarse_cache = mlp_forward(
        coarse_inputs,
        coarse_latents.astype(jnp.float32),
        node_weight_in,
        node_weight_out,
        node_gain,
    )
    coarse_grad_inputs, coarse_first, coarse_second, coarse_gain_grad = mlp_backward(
        coarse_inputs,
        node_weight_in,
        node_weight_out,
        node_gain,
        coarse_cache,
        coarse_cotangent.astype(jnp.float32),
    )
    coarse_grad = coarse_grad_inputs[:, latent_width:]
    coarse_after = coarse_cotangent.astype(jnp.float32) + coarse_grad_inputs[:, :latent_width]
    node_first_total, node_second_total, node_gain_total = (node_first, node_second, node_gain_grad)
    extra_first, extra_second, extra_gain = (coarse_first, coarse_second, coarse_gain_grad)
    up_cotangent = ups_cotangent.astype(jnp.float32) + jnp.take(coarse_grad, up_receiver, axis=0)
    up_grad_inputs, up_first, up_second, up_gain_grad = mlp_backward(
        up_inputs, edge_weight_in, edge_weight_out, edge_gain, up_cache, up_cotangent
    )
    grad_ups = up_cotangent + up_grad_inputs[:, :latent_width]
    fine_grad = node_grad_inputs[:, latent_width:]
    edge_cotangent = edges_cotangent.astype(jnp.float32) + jnp.take(
        fine_grad, edge_receiver, axis=0
    )
    edge_grad_inputs, edge_first, edge_second, edge_gain_grad = mlp_backward(
        edge_inputs, edge_weight_in, edge_weight_out, edge_gain, edge_cache, edge_cotangent
    )
    grad_edges = edge_cotangent + edge_grad_inputs[:, :latent_width]
    table_grad = jax.ops.segment_sum(
        edge_grad_inputs[:, latent_width : 2 * latent_width],
        edge_sender,
        num_segments=node_count + import_count + coarse_count,
    )
    returning = table_grad[node_count : node_count + import_count].reshape(
        devices, slot_count, latent_width
    )
    face_count = lax.axis_size("face")
    sectioned_back = returning.reshape(face_count, devices // face_count, slot_count, latent_width)
    returned = lax.all_to_all(
        lax.all_to_all(
            sectioned_back.astype(jnp.bfloat16), "face", split_axis=0, concat_axis=0, tiled=True
        ),
        "band",
        split_axis=1,
        concat_axis=1,
        tiled=True,
    ).astype(sectioned_back.dtype)
    grad_nodes = (
        nodes_cotangent.astype(jnp.float32)
        + node_grad_inputs[:, :latent_width]
        + table_grad[:node_count]
        + jax.ops.segment_sum(
            edge_grad_inputs[:, 2 * latent_width :], edge_receiver, num_segments=node_count
        )
        + jax.ops.segment_sum(
            up_grad_inputs[:, latent_width : 2 * latent_width], up_sender, num_segments=node_count
        )
        + jax.ops.segment_sum(
            returned.reshape(import_count, latent_width),
            send_table.reshape(import_count),
            num_segments=node_count,
        )
    )
    coarse_local = table_grad[node_count + import_count :] + jax.ops.segment_sum(
        up_grad_inputs[:, 2 * latent_width :], up_receiver, num_segments=coarse_count
    )
    edge_first_total = edge_first + up_first
    edge_second_total = edge_second + up_second
    edge_gain_total = edge_gain_grad + up_gain_grad
    summed = lax.psum(
        (
            node_first_total,
            node_second_total,
            node_gain_total,
            coarse_local,
            edge_first_total,
            edge_second_total,
            edge_gain_total,
        ),
        ("face", "band"),
    )
    node_summed = (summed[0], summed[1], summed[2])
    edge_summed = (summed[3], summed[4], summed[5], summed[6])
    edge_rows_total = (edge_latents.shape[0] + up_latents.shape[0]) * devices
    node_rows_total = node_count * devices + coarse_count
    edge_scale = 1.0 / math.sqrt(edge_rows_total)
    node_scale = 1.0 / math.sqrt(node_rows_total)
    grad_coarse = edge_summed[0] + coarse_after
    return (
        grad_nodes,
        grad_coarse,
        grad_edges,
        grad_ups,
        edge_summed[1] * edge_scale,
        edge_summed[2] * edge_scale,
        edge_summed[3] * edge_scale,
        (node_summed[0] + extra_first) * node_scale,
        (node_summed[1] + extra_second) * node_scale,
        (node_summed[2] + extra_gain) * node_scale,
    )


def solution(mesh):
    return jax.shard_map(
        per_device,
        mesh=mesh,
        in_specs=(
            P(("face", "band"), None),
            P(),
            P(("face", "band"), None),
            P(("face", "band"), None),
            P(),
            P(),
            P(),
            P(),
            P(),
            P(),
            P(("face", "band"), None),
            P(),
            P(("face", "band"), None),
            P(("face", "band"), None),
            P(("face", "band"), None, None),
            P(("face", "band")),
            P(("face", "band")),
            P(("face", "band")),
            P(("face", "band")),
        ),
        out_specs=(
            P(("face", "band"), None),
            P(),
            P(("face", "band"), None),
            P(("face", "band"), None),
            P(),
            P(),
            P(),
            P(),
            P(),
            P(),
        ),
        check_vma=False,
    )
```

profile of v0, /device:TPU:0, one launch (start us, length us, event | category | flops | bytes accessed | tf_op | source)
XLA Modules:
  0.0 415.9 jit_solution(11921928592498029254)
XLA Ops:
  11.9 7.3 %all-to-all-start = ((bf16[8,4,4,512]{3,2,1,0:T(4,128)(2,1)}), bf16[8,4,4,512]{3,2,1,0:T(4,128)(2,1)}, u32[]{:S(2)}, u32[]{:S(2)}) async-start(bf16[8,4,4,512]{3,2,1,0:T(4,128)(2,1)} %broadcast_select_fusion.4), calls=%async_computation | async-start | bytes 262144 | tf_op jit(solution)/shard_map/all_to_all | solution.py:72
  29.2 62.0 %all-reduce.6 = bf16[1024,512]{1,0:T(8,128)(2,1)} all-reduce(f32[1024,512]{1,0:T(8,128)} %fusion.22), channel_id=1, replica_groups=mesh['face'=8,'band'=4] {'face','band'}, use_global_device_ids=true, to_apply=%region_12.13 | all-reduce | flops 524288 | bytes 3145728 | tf_op jit(solution)/shard_map/psum | solution.py:123
  96.3 3.0 copy.111
  120.9 3.3 all-to-all-start.1
  126.3 4.0 gather_fusion.2
  136.0 5.1 %gather_fusion.1 = bf16[1024,512]{1,0:T(8,128)(2,1)} fusion(bf16[1408,512]{1,0:T(8,128)(2,1)S(1)} %pad_maximum_fusion.2, s32[1024]{0:T(1024)S(1)} %fusion.45), kind=kCustom, calls=%fused_computation.1 | custom fusion | bytes 2101248 | tf_op jit(solution)/shard_map/jit(_take)/gather | solution.py:84
  156.6 4.9 %gather_fusion.3 = f32[1024,512]{1,0:T(8,128)} fusion(f32[256,512]{1,0:T(8,128)S(1)} %slice.68, s32[1024]{0:T(1024)S(1)} %fusion.46), kind=kCustom, calls=%fused_computation.3 | custom fusion | bytes 4198400 | tf_op jit(solution)/shard_map/jit(_take)/gather | solution.py:152
  161.5 3.2 copy.110
  164.7 3.3 multiply_reduce_fusion
  174.3 4.5 %fusion.68 = f32[1024,1536]{1,0:T(8,128)} fusion(bf16[1024,512]{1,0:T(8,128)(2,1)S(1)} %multiply_convert_fusion.2, bf16[1536,512]{1,0:T(8,128)(2,1)S(1)} %copy-done), kind=kOutput, calls=%fused_computation.170 | convolution fusion | flops 1610612736 | bytes 8912896 | tf_op jit(solution)/shard_map/dot_general | solution.py:36
  182.8 9.1 %scatter_custom_fusion = f32[1408,512]{1,0:T(8,128)} fusion(s32[1024]{0:T(1024)} %param.34, f32[1024,1536]{1,0:T(8,128)} %fusion.68, f32[]{:T(128)} %constant.129.clone.1), kind=kCustom, calls=%fused_computation.28 | custom fusion | flops 524288 | bytes 4981248 | tf_op jit(solution)/shard_map/scatter-add | solution.py:159
  191.9 3.2 slice.75
  195.1 5.1 %scatter_custom_fusion.4 = f32[1024,512]{1,0:T(8,128)} fusion(f32[1024,512]{1,0:T(8,128)} %slice.75, s32[256]{0:T(256)} %param.37, f32[256,1536]{1,0:T(8,128)S(1)} %copy-done.11), kind=kCustom, calls=%fused_computation.83 | custom fusion | flops 131072 | bytes 2621440 | tf_op jit(solution)/shard_map/scatter-add | solution.py:194
  201.0 3.3 scatter_custom_fusion.2
  208.0 4.4 %all-to-all-start.2 = ((bf16[8,4,4,512]{3,2,1,0:T(4,128)(2,1)}), bf16[8,4,4,512]{3,2,1,0:T(4,128)(2,1)S(1)}, u32[]{:S(2)}, u32[]{:S(2)}) async-start(bf16[8,4,4,512]{3,2,1,0:T(4,128)(2,1)} %convert_element_type.97), calls=%async_computation.2 | async-start | bytes 262144 | tf_op jit(solution)/shard_map/all_to_all | solution.py:170
  213.9 42.8 %all-reduce = (f32[512]{0:T(512)S(1)}, f32[512]{0:T(512)S(1)}) all-reduce(f32[512]{0:T(512)S(1)} %add.244, f32[512]{0:T(512)S(1)} %copy-done.51), channel_id=1, replica_groups=mesh['face'=8,'band'=4] {'face','band'}, use_global_device_ids=true, to_apply=%region_27.28 | all-reduce | flops 1024 | bytes 8192 | tf_op jit(solution)/shard_map/psum | solution.py:200
  257.9 3.5 all-to-all-start.3
  262.0 3.3 slice.78
  265.3 2.9 copy.118
  268.2 4.1 add.240
  272.3 2.9 copy.117
  275.2 7.6 %scatter_custom_fusion.1 = f32[256,512]{1,0:T(8,128)S(1)} fusion(f32[256,512]{1,0:T(8,128)S(1)} %fusion.30, s32[1024]{0:T(1024)S(1)} %copy-done.48, f32[1024,1536]{1,0:T(8,128)} %fusion.68), kind=kCustom, calls=%fused_computation.26 | custom fusion | flops 524288 | bytes 2621440 | tf_op jit(solution)/shard_map/scatter-add | solution.py:182
  284.9 111.1 %all-reduce.5.cloned.1.call-done = (f32[1024,512]{1,0:T(8,128)}, f32[1536,512]{1,0:T(8,128)}, f32[512,512]{1,0:T(8,128)}, f32[1024,512]{1,0:T(8,128)}, f32[512,512]{1,0:T(8,128)}) async-done(((f32[1024,512]{1,0:T(8,128)}, f32[1536,512]{1,0:T(8,128)}, f32[512,512]{1,0:T(8,128)}, f32[1024,512]{1,0:T(8,128)}, f32[512,512]{1,0:T(8,128)}), (f32[1024,512]{1,0:T(8,128)}, f32[1536,512]{1,0:T(8,128)}, ...) | async-done | bytes 9437200 | tf_op jit(solution)/shard_map/psum | solution.py:200
  396.0 3.8 fusion.14
  (253 shorter events, 93.0 us)
Async XLA Ops:
  7.2 17.3 %copy-start = (bf16[1536,512]{1,0:T(8,128)(2,1)S(1)}, bf16[1536,512]{1,0:T(8,128)(2,1)}, u32[]{:S(2)}) copy-start(bf16[1536,512]{1,0:T(8,128)(2,1)} %param.23) | copy-start | bytes 4718596
  7.2 14.7 %copy-start.1 = (bf16[256,512]{1,0:T(8,128)(2,1)S(1)}, bf16[256,512]{1,0:T(8,128)(2,1)}, u32[]{:S(2)}) copy-start(bf16[256,512]{1,0:T(8,128)(2,1)} %param.19) | copy-start | bytes 786436
  11.0 12.1 %copy-start.9 = (bf16[1024,512]{1,0:T(8,128)(2,1)S(1)}, bf16[1024,512]{1,0:T(8,128)(2,1)}, u32[]{:S(2)}) copy-start(bf16[1024,512]{1,0:T(8,128)(2,1)} %param.20) | copy-start | bytes 3145732
  11.9 107.4 %all-to-all-start = ((bf16[8,4,4,512]{3,2,1,0:T(4,128)(2,1)}), bf16[8,4,4,512]{3,2,1,0:T(4,128)(2,1)}, u32[]{:S(2)}, u32[]{:S(2)}) async-start(bf16[8,4,4,512]{3,2,1,0:T(4,128)(2,1)} %broadcast_select_fusion.4), calls=%async_computation | async-start | bytes 262144 | tf_op jit(solution)/shard_map/all_to_all | solution.py:72
  96.3 5.1 %copy-start.7 = (bf16[1024,512]{1,0:T(8,128)(2,1)S(1)}, bf16[1024,512]{1,0:T(8,128)(2,1)}, u32[]{:S(2)}) copy-start(bf16[1024,512]{1,0:T(8,128)(2,1)} %param.30) | copy-start | bytes 3145732
  116.9 8.1 %copy-start.28 = (bf16[1024,512]{1,0:T(8,128)(2,1)S(1)}, bf16[1024,512]{1,0:T(8,128)(2,1)}, u32[]{:S(2)}) copy-start(bf16[1024,512]{1,0:T(8,128)(2,1)} %param.21) | copy-start | bytes 3145732
  120.9 13.0 %all-to-all-start.1 = ((bf16[8,4,4,512]{3,2,0,1:T(4,128)(2,1)}), bf16[8,4,4,512]{3,2,0,1:T(4,128)(2,1)S(1)}, u32[]{:S(2)}, u32[]{:S(2)}) async-start(bf16[8,4,4,512]{3,2,0,1:T(4,128)(2,1)} %copy.104), calls=%async_computation.1 | async-start | bytes 262144 | tf_op jit(solution)/shard_map/all_to_all | solution.py:71
  124.2 271.8 %all-reduce.5.cloned.1.call-start = ((), (), s32[]{:S(2)}) async-start(), calls=%async_computation.4 | async-start | bytes 18874368 | tf_op jit(solution)/shard_map/psum | solution.py:200
  174.2 4.5 %copy-start.25 = (bf16[256,512]{1,0:T(8,128)(2,1)S(1)}, bf16[256,512]{1,0:T(8,128)(2,1)}, u32[]{:S(2)}) copy-start(bf16[256,512]{1,0:T(8,128)(2,1)} %copy-done.24) | copy-start | bytes 786436
  174.2 4.5 %copy-start.27 = (bf16[256,512]{1,0:T(8,128)(2,1)S(1)}, bf16[256,512]{1,0:T(8,128)(2,1)}, u32[]{:S(2)}) copy-start(bf16[256,512]{1,0:T(8,128)(2,1)} %copy-done.26) | copy-start | bytes 786436
  174.2 4.5 %copy-start.41 = (bf16[256,512]{1,0:T(8,128)(2,1)S(1)}, bf16[256,512]{1,0:T(8,128)(2,1)}, u32[]{:S(2)}) copy-start(bf16[256,512]{1,0:T(8,128)(2,1)} %param.22) | copy-start | bytes 786436
  200.9 11.6 %copy-start.23 = (bf16[256,512]{1,0:T(8,128)(2,1)S(1)}, bf16[256,512]{1,0:T(8,128)(2,1)}, u32[]{:S(2)}) copy-start(bf16[256,512]{1,0:T(8,128)(2,1)} %param.29) | copy-start | bytes 786436
  204.3 9.5 %copy-start.52 = (f32[512]{0:T(512)S(1)}, f32[512]{0:T(512)}, u32[]{:S(2)}) copy-start(f32[512]{0:T(512)} %get-tuple-element.76) | copy-start | bytes 6148
  204.4 9.5 %copy-start.51 = (f32[512]{0:T(512)S(1)}, f32[512]{0:T(512)}, u32[]{:S(2)}) copy-start(f32[512]{0:T(512)} %get-tuple-element.78) | copy-start | bytes 6148
  204.4 52.2 %copy-start.50 = (f32[512]{0:T(512)S(1)}, f32[512]{0:T(512)}, u32[]{:S(2)}) copy-start(f32[512]{0:T(512)} %get-tuple-element.72) | copy-start | bytes 6148
  208.0 49.2 %all-to-all-start.2 = ((bf16[8,4,4,512]{3,2,1,0:T(4,128)(2,1)}), bf16[8,4,4,512]{3,2,1,0:T(4,128)(2,1)S(1)}, u32[]{:S(2)}, u32[]{:S(2)}) async-start(bf16[8,4,4,512]{3,2,1,0:T(4,128)(2,1)} %convert_element_type.97), calls=%async_computation.2 | async-start | bytes 262144 | tf_op jit(solution)/shard_map/all_to_all | solution.py:170
  257.9 25.1 %all-to-all-start.3 = ((bf16[8,4,4,512]{3,2,0,1:T(4,128)(2,1)}), bf16[8,4,4,512]{3,2,0,1:T(4,128)(2,1)S(1)}, u32[]{:S(2)}, u32[]{:S(2)}) async-start(bf16[8,4,4,512]{3,2,0,1:T(4,128)(2,1)} %copy.113), calls=%async_computation.3 | async-start | bytes 262144 | tf_op jit(solution)/shard_map/all_to_all | solution.py:169
  275.2 7.7 %copy-start.20 = (f32[256,512]{1,0:T(8,128)S(1)}, f32[256,512]{1,0:T(8,128)}, u32[]{:S(2)}) copy-start(f32[256,512]{1,0:T(8,128)} %scatter_custom_fusion.2) | copy-start | bytes 1572868
  283.3 112.7 %copy-start.35 = (bf16[1024,512]{1,0:T(8,128)(2,1)S(1)}, bf16[1024,512]{1,0:T(8,128)(2,1)}, u32[]{:S(2)}) copy-start(bf16[1024,512]{1,0:T(8,128)(2,1)} %copy-done.34) | copy-start | bytes 3145732
  284.9 114.9 %copy-start.6 = (f32[256,512]{1,0:T(8,128)}, f32[256,512]{1,0:T(8,128)S(1)}, u32[]{:S(2)}) copy-start(f32[256,512]{1,0:T(8,128)S(1)} %scatter_fusion) | copy-start | bytes 1572868
  396.0 3.8 copy-start.21
  396.0 3.8 copy-start.55
  396.0 3.8 copy-start.64
  399.9 3.9 copy-start.19
  (53 other events, 98.5 us)
Sparse Core Ops, SparseCore 0:
  200.3 195.6 all-reduce.4
where the time goes:
time: 421 us; the launch traced here: 416 us
  waiting for transfers between devices  111 us (26%)
  blocking collectives  105 us (25%)
  local copies, waits for them, and re-layouts  64.5 us (15%)
  other arithmetic  60 us (14%)
  matrix products  41.4 us (10%)
  starting transfers between devices  18.8 us (4%)
  between operations  15.2 us (4%)
    psum x1, waiting for transfers between devices, per_device(): lax.psum((node_first_total, node_second_total, node_gain_total, coarse_lo...  111 us
    psum x1, blocking collectives, per_device(): lax.psum(jnp.dot(onehot_rows, new_ups, preferred_element_type=jnp.float32...  62 us
    psum x1, blocking collectives, per_device(): lax.psum((node_first_total, node_second_total, node_gain_total, coarse_lo...  42.8 us
    unnamed x149, local copies, waits for them, and re-layouts  19.5 us
    scatter-add x1, other arithmetic, per_device(): jax.ops.segment_sum(edge_grad_inputs[:, latent_width:2 * latent_width], e...  9.1 us
    dot_general x4, matrix products, mlp_backward(): grad_first = jnp.dot(inputs.T, grad_pre, preferred_element_type=jnp.float32)  8.44 us
  transfers between devices with their start and end apart: 5, of which 1 were waited for; matrix products, arithmetic and copies ran while one was open for 18% of the time, Pallas kernels for 0%

commit v1 on v0

v1 whole, which is shorter than its diff:
```python
import functools
import math

import jax
import jax.numpy as jnp
from jax import lax
from jax.experimental import pallas as pl
from jax.experimental.pallas import tpu as pltpu
from jax.sharding import Mesh, PartitionSpec as P

EPSILON = 1e-05
BF = jnp.bfloat16
F32 = jnp.float32
VMEM_LIMIT = 56 * 1024 * 1024


def dot(a, b):
    return lax.dot_general(a, b, (((1,), (0,)), ((), ())), preferred_element_type=F32)


def dot_lt(a, b):
    return lax.dot_general(a, b, (((0,), (0,)), ((), ())), preferred_element_type=F32)


def dot_rt(a, b):
    return lax.dot_general(a, b, (((1,), (1,)), ((), ())), preferred_element_type=F32)


def onehot_t(index_row, rows, offset=0):
    ids = lax.broadcasted_iota(jnp.int32, (rows, index_row.shape[1]), 0) + offset
    return jnp.where(ids == index_row, 1.0, 0.0).astype(BF)


def hidden_of(pre):
    return (pre * jax.nn.sigmoid(pre)).astype(BF)


def normalise(projected):
    center = projected - jnp.mean(projected, axis=1, keepdims=True)
    inv_std = lax.rsqrt(jnp.mean(center * center, axis=1, keepdims=True) + EPSILON)
    return center * inv_std, inv_std


def grad_to_pre(pre, hidden, normed, inv_std, cot, gain, w2):
    gain_part = jnp.sum(cot * normed, axis=0, keepdims=True)
    scaled = cot * gain
    d_proj = (
        inv_std
        * (
            scaled
            - jnp.mean(scaled, axis=1, keepdims=True)
            - normed * jnp.mean(scaled * normed, axis=1, keepdims=True)
        )
    ).astype(BF)
    d_hidden = dot_rt(d_proj, w2)
    logistic = jax.nn.sigmoid(pre)
    d_pre = (d_hidden * logistic * (1.0 + pre * (1.0 - logistic))).astype(BF)
    return gain_part, d_proj, d_pre


def gather_f32(onehot, table):
    high = table.astype(BF)
    low = (table - high.astype(F32)).astype(BF)
    return dot_lt(onehot, high) + dot_lt(onehot, low)


def up_forward_kernel(us, ur, up, node, coarse, w1, w2, gain, p_ref, xs_ref, xr_ref, part_ref):
    lat = up.shape[1]
    xs = dot_lt(onehot_t(us[...], node.shape[0]), node[...]).astype(BF)
    hot_r = onehot_t(ur[...], coarse.shape[0])
    xr = dot_lt(hot_r, coarse[...]).astype(BF)
    pre = dot(up[...], w1[0:lat]) + dot(xs, w1[lat : 2 * lat]) + dot(xr, w1[2 * lat :])
    normed, _ = normalise(dot(hidden_of(pre), w2[...]))
    new = (up[...].astype(F32) + normed * gain[...]).astype(BF)
    p_ref[...] = pre
    xs_ref[...] = xs
    xr_ref[...] = xr
    part_ref[...] = dot(hot_r, new).astype(BF)


def edge_forward_kernel(
    es, er, edge, node, halo, coarse, w1, w2, gain, nw1, nw2, ngain, ncot,
    p_ref, xs_ref, fg_ref, gn_ref, ngw1_ref, ngw2_ref, ngg_ref, acc,
):
    step = pl.program_id(0)
    lat = edge.shape[1]
    n = node.shape[0]
    imports = halo.shape[0]

    @pl.when(step == 0)
    def _():
        acc[...] = jnp.zeros_like(acc)

    sender = es[...]
    xs = (
        dot_lt(onehot_t(sender, n), node[...])
        + dot_lt(onehot_t(sender, imports, n), halo[...])
        + dot_lt(onehot_t(sender, coarse.shape[0], n + imports), coarse[...])
    ).astype(BF)
    hot_r = onehot_t(er[...], n)
    xr = dot_lt(hot_r, node[...]).astype(BF)
    pre = dot(edge[...], w1[0:lat]) + dot(xs, w1[lat : 2 * lat]) + dot(xr, w1[2 * lat :])
    normed, _ = normalise(dot(hidden_of(pre), w2[...]))
    new = (edge[...].astype(F32) + normed * gain[...]).astype(BF)
    p_ref[...] = pre
    xs_ref[...] = xs
    acc[...] += dot(hot_r, new)

    @pl.when(step == pl.num_programs(0) - 1)
    def _():
        total = acc[...].astype(BF)
        node_pre = dot(node[...], nw1[0:lat]) + dot(total, nw1[lat:])
        hidden = hidden_of(node_pre)
        node_normed, inv_std = normalise(dot(hidden, nw2[...]))
        cot = ncot[...].astype(F32)
        gain_part, d_proj, d_pre = grad_to_pre(
            node_pre, hidden, node_normed, inv_std, cot, ngain[...], nw2[...]
        )
        ngg_ref[...] = gain_part
        ngw2_ref[...] = dot_lt(hidden, d_proj)
        ngw1_ref[0:lat] = dot_lt(node[...], d_pre)
        ngw1_ref[lat:] = dot_lt(total, d_pre)
        gn_ref[...] = cot + dot_rt(d_pre, nw1[0:lat])
        fg_ref[...] = dot_rt(d_pre, nw1[lat:])


def edge_backward_kernel(
    es, er, edge, xs, pre_ref, ecot, fg, node, w1, w2, gain,
    ge_ref, gw1_ref, gw2_ref, gg_ref, np_ref, ret_ref, cp_ref, sum_s, sum_r,
):
    step = pl.program_id(0)
    lat = edge.shape[1]
    n = node.shape[0]
    imports = ret_ref.shape[0]

    @pl.when(step == 0)
    def _():
        sum_s[...] = jnp.zeros_like(sum_s)
        sum_r[...] = jnp.zeros_like(sum_r)
        gw1_ref[...] = jnp.zeros_like(gw1_ref)
        gw2_ref[...] = jnp.zeros_like(gw2_ref)
        gg_ref[...] = jnp.zeros_like(gg_ref)

    hot_r = onehot_t(er[...], n)
    cot = ecot[...].astype(F32) + gather_f32(hot_r, fg[...])
    pre = pre_ref[...]
    hidden = hidden_of(pre)
    normed, inv_std = normalise(dot(hidden, w2[...]))
    gain_part, d_proj, d_pre = grad_to_pre(pre, hidden, normed, inv_std, cot, gain[...], w2[...])
    gg_ref[...] += gain_part
    gw2_ref[...] += dot_lt(hidden, d_proj)
    gw1_ref[0:lat] += dot_lt(edge[...], d_pre)
    gw1_ref[lat : 2 * lat] += dot_lt(xs[...], d_pre)
    ge_ref[...] = cot + dot_rt(d_pre, w1[0:lat])
    sum_r[...] += dot(hot_r, d_pre)
    sum_s[...] += dot(onehot_t(es[...], sum_s.shape[0]), d_pre)

    @pl.when(step == pl.num_programs(0) - 1)
    def _():
        w_s = w1[lat : 2 * lat]
        recv = sum_r[...].astype(BF)
        gw1_ref[2 * lat :] = dot_lt(node[...], recv)
        np_ref[...] = dot_rt(sum_s[0:n].astype(BF), w_s) + dot_rt(recv, w1[2 * lat :])
        ret_ref[...] = dot_rt(sum_s[n : n + imports].astype(BF), w_s).astype(BF)
        cp_ref[...] = dot_rt(sum_s[n + imports :].astype(BF), w_s)


def coarse_kernel(
    rows, total_in, ccot, nw1, nw2, ngain, ngw1, ngw2, ngg, cg_ref, after_ref, pay_ref, gg_ref
):
    lat = rows.shape[1]
    total = total_in[...].astype(BF)
    pre = dot(rows[...], nw1[0:lat]) + dot(total, nw1[lat:])
    hidden = hidden_of(pre)
    normed, inv_std = normalise(dot(hidden, nw2[...]))
    cot = ccot[...].astype(F32)
    gain_part, d_proj, d_pre = grad_to_pre(pre, hidden, normed, inv_std, cot, ngain[...], nw2[...])
    cg_ref[...] = dot_rt(d_pre, nw1[lat:]).astype(BF)
    after_ref[...] = cot + dot_rt(d_pre, nw1[0:lat])
    pay_ref[0:lat] = (ngw1[0:lat] + dot_lt(rows[...], d_pre)).astype(BF)
    pay_ref[lat : 2 * lat] = (ngw1[lat:] + dot_lt(total, d_pre)).astype(BF)
    pay_ref[2 * lat :] = (ngw2[...] + dot_lt(hidden, d_proj)).astype(BF)
    gg_ref[...] = ngg[...] + gain_part


def up_backward_kernel(
    us, ur, own, up, xs, xr, pre_ref, ucot, cg, w1, w2, gain, gw1, gw2, gg, cp, after,
    gu_ref, np_ref, pay_ref, ggo_ref, csum,
):
    lat = up.shape[1]
    width = gw2.shape[0]
    coarse = cg.shape[0]
    hot_r = onehot_t(ur[...], coarse)
    cot = ucot[...].astype(F32) + dot_lt(hot_r, cg[...])
    pre = pre_ref[...]
    hidden = hidden_of(pre)
    normed, inv_std = normalise(dot(hidden, w2[...]))
    gain_part, d_proj, d_pre = grad_to_pre(pre, hidden, normed, inv_std, cot, gain[...], w2[...])
    ggo_ref[...] = gg[...] + gain_part
    gu_ref[...] = cot + dot_rt(d_pre, w1[0:lat])
    send = dot(onehot_t(us[...], np_ref.shape[0]), d_pre).astype(BF)
    np_ref[...] = dot_rt(send, w1[lat : 2 * lat])
    csum[...] = cp[...] + dot_rt(dot(hot_r, d_pre).astype(BF), w1[2 * lat :])
    count = after.shape[0]
    mine = pl.ds(pl.multiple_of(own[0] * count, 8), count)
    csum[mine, :] = csum[mine, :] + after[...]
    pay_ref[0:coarse] = csum[...].astype(BF)
    pay_ref[coarse : coarse + lat] = (gw1[0:lat] + dot_lt(up[...], d_pre)).astype(BF)
    pay_ref[coarse + lat : coarse + 2 * lat] = (
        gw1[lat : 2 * lat] + dot_lt(xs[...], d_pre)
    ).astype(BF)
    pay_ref[coarse + 2 * lat : coarse + 3 * lat] = (
        gw1[2 * lat :] + dot_lt(xr[...], d_pre)
    ).astype(BF)
    pay_ref[coarse + 3 * lat :] = (gw2[...] + dot_lt(hidden, d_proj)).astype(BF)


def params(*semantics):
    return pltpu.CompilerParams(
        dimension_semantics=semantics or None, vmem_limit_bytes=VMEM_LIMIT
    )


def shape(rows, cols, dtype):
    return jax.ShapeDtypeStruct((rows, cols), dtype)


def whole(arr):
    return pl.BlockSpec(arr.shape, lambda i: (0,) * len(arr.shape))


def swap(x, axes, count):
    if count == 1:
        return x
    return lax.all_to_all(x, axes, 0, 0, tiled=True)


GROUPS = ("core", ("x", "y"), "z")


def group_sizes():
    return tuple(lax.axis_size(axes) for axes in GROUPS)


def owner_index():
    index = jnp.int32(0)
    for axes in GROUPS:
        index = index * lax.axis_size(axes) + lax.axis_index(axes)
    return index


def reduce_scatter(x):
    for axes in GROUPS:
        count = lax.axis_size(axes)
        got = swap(x.astype(BF), axes, count)
        x = jnp.sum(got.reshape(count, -1, x.shape[1]).astype(F32), axis=0)
    return x


def all_gather(x):
    for axes in reversed(GROUPS):
        count = lax.axis_size(axes)
        copies = jnp.broadcast_to(x[None], (count,) + x.shape).reshape(-1, x.shape[1])
        x = swap(copies, axes, count)
    return x


def sum_rows_everywhere(x):
    for axes in GROUPS:
        count = lax.axis_size(axes)
        copies = jnp.broadcast_to(x[None], (count,) + x.shape).reshape(-1, x.shape[1])
        x = jnp.sum(swap(copies, axes, count).reshape(count, -1, x.shape[1]), axis=0)
    return x


def reduce_everywhere(payload):
    devices = math.prod(group_sizes())
    rows = payload.shape[0]
    padded = -(-rows // (16 * devices)) * 16 * devices
    if padded > rows:
        payload = jnp.pad(payload, ((0, padded - rows), (0, 0)))
    return all_gather(reduce_scatter(payload).astype(BF))[:rows]


def per_device(
    node, coarse, edge, up, w1, w2, gain, nw1, nw2, ngain, ncot, ccot, ecot, ucot,
    send_rows, edge_sender, edge_receiver, up_sender, up_receiver,
):
    n, lat = node.shape
    width = w2.shape[0]
    ccount = coarse.shape[0]
    ecount = edge.shape[0]
    ucount = up.shape[0]
    devices, slots = send_rows.shape[1], send_rows.shape[2]
    imports = devices * slots
    everyone = ("z", "x", "y", "core")
    es, er = edge_sender.reshape(1, ecount), edge_receiver.reshape(1, ecount)
    us, ur = up_sender.reshape(1, ucount), up_receiver.reshape(1, ucount)
    gain_row, ngain_row = gain.reshape(1, lat), ngain.reshape(1, lat)
    own = owner_index()

    table = send_rows.reshape(imports)
    hot_send = (table[:, None] == jnp.arange(n, dtype=jnp.int32)[None, :]).astype(BF)
    outgoing = dot(hot_send, node).astype(BF)
    halo = lax.all_to_all(
        outgoing.reshape(devices, slots, lat), everyone, 0, 0, tiled=True
    ).reshape(imports, lat)

    up_pre, up_xs, up_xr, coarse_part = pl.pallas_call(
        up_forward_kernel,
        out_shape=(
            shape(ucount, width, F32), shape(ucount, lat, BF), shape(ucount, lat, BF),
            shape(ccount, lat, BF),
        ),
        compiler_params=params(),
        name="up_forward",
    )(us, ur, up, node, coarse, w1, w2, gain_row)

    coarse_total = reduce_scatter(coarse_part)

    tile = math.gcd(ecount, 256)
    steps = ecount // tile
    rows_spec = pl.BlockSpec((tile, lat), lambda i: (i, 0))
    index_spec = pl.BlockSpec((1, tile), lambda i: (0, i))
    fixed = lambda r, c: pl.BlockSpec((r, c), lambda i: (0, 0))
    pre, xs, fine_grad, grad_n, ngw1, ngw2, ngg = pl.pallas_call(
        edge_forward_kernel,
        grid=(steps,),
        in_specs=[index_spec, index_spec, rows_spec]
        + [whole(a) for a in (node, halo, coarse, w1, w2, gain_row, nw1, nw2, ngain_row, ncot)],
        out_specs=[
            pl.BlockSpec((tile, width), lambda i: (i, 0)), rows_spec, fixed(n, lat), fixed(n, lat),
            fixed(2 * lat, width), fixed(width, lat), fixed(1, lat),
        ],
        out_shape=(
            shape(ecount, width, F32), shape(ecount, lat, BF), shape(n, lat, F32),
            shape(n, lat, F32), shape(2 * lat, width, F32), shape(width, lat, F32),
            shape(1, lat, F32),
        ),
        scratch_shapes=[pltpu.VMEM((n, lat), F32)],
        compiler_params=params("arbitrary"),
        name="edge_forward",
    )(es, er, edge, node, halo, coarse, w1, w2, gain_row, nw1, nw2, ngain_row, ncot)

    grad_e, gw1, gw2, gg, node_part, returning, coarse_local = pl.pallas_call(
        edge_backward_kernel,
        grid=(steps,),
        in_specs=[
            index_spec, index_spec, rows_spec, rows_spec,
            pl.BlockSpec((tile, width), lambda i: (i, 0)), rows_spec,
        ]
        + [whole(a) for a in (fine_grad, node, w1, w2, gain_row)],
        out_specs=[
            rows_spec, fixed(3 * lat, width), fixed(width, lat), fixed(1, lat), fixed(n, lat),
            fixed(imports, lat), fixed(ccount, lat),
        ],
        out_shape=(
            shape(ecount, lat, F32), shape(3 * lat, width, F32), shape(width, lat, F32),
            shape(1, lat, F32), shape(n, lat, F32), shape(imports, lat, BF),
            shape(ccount, lat, F32),
        ),
        scratch_shapes=[
            pltpu.VMEM((n + imports + ccount, width), F32), pltpu.VMEM((n, width), F32),
        ],
        compiler_params=params("arbitrary"),
        name="edge_backward",
    )(es, er, edge, xs, pre, ecot, fine_grad, node, w1, w2, gain_row)

    returned = lax.all_to_all(
        returning.reshape(devices, slots, lat), everyone, 0, 0, tiled=True
    ).reshape(imports, lat)

    mine = ccount // devices
    padded = -(-mine // 16) * 16
    pad = lambda a: jnp.pad(a, ((0, padded - mine), (0, 0))) if padded > mine else a
    own_coarse = pad(lax.dynamic_slice_in_dim(coarse, own * mine, mine, 0))
    own_cot = pad(lax.dynamic_slice_in_dim(ccot, own * mine, mine, 0))
    coarse_grad, coarse_after, node_pay, ngg_sum = pl.pallas_call(
        coarse_kernel,
        out_shape=(
            shape(padded, lat, BF), shape(padded, lat, F32), shape(2 * lat + width, lat, BF),
            shape(1, lat, F32),
        ),
        compiler_params=params(),
        name="coarse_mlp",
    )(own_coarse, pad(coarse_total), own_cot, nw1, nw2, ngain_row, ngw1, ngw2, ngg)
    coarse_grad_all = all_gather(coarse_grad[:mine])

    node_total = reduce_everywhere(node_pay)

    grad_u, up_node_part, edge_pay, gg_sum = pl.pallas_call(
        up_backward_kernel,
        in_specs=[pl.BlockSpec(memory_space=pltpu.VMEM)] * 2
        + [pl.BlockSpec(memory_space=pltpu.SMEM)]
        + [pl.BlockSpec(memory_space=pltpu.VMEM)] * 14,
        out_shape=(
            shape(ucount, lat, F32), shape(n, lat, F32),
            shape(ccount + 3 * lat + width, lat, BF), shape(1, lat, F32),
        ),
        scratch_shapes=[pltpu.VMEM((ccount, lat), F32)],
        compiler_params=params(),
        name="up_backward",
    )(
        us, ur, own.reshape(1), up, up_xs, up_xr, up_pre, ucot, coarse_grad_all, w1, w2, gain_row,
        gw1, gw2, gg, coarse_local, coarse_after[:mine],
    )
    edge_total = reduce_everywhere(edge_pay)
    gains = sum_rows_everywhere(jnp.concatenate([gg_sum, ngg_sum], 0))

    grad_nodes = (
        grad_n
        + node_part
        + up_node_part
        + lax.dot_general(hot_send, returned, (((0,), (0,)), ((), ())), preferred_element_type=F32)
    )
    edge_scale = 1.0 / math.sqrt((ecount + ucount) * devices)
    node_scale = 1.0 / math.sqrt(n * devices + ccount)
    in_end = ccount + 3 * lat
    return (
        grad_nodes,
        edge_total[:ccount].astype(F32),
        grad_e,
        grad_u,
        edge_total[ccount:in_end].astype(F32) * edge_scale,
        edge_total[in_end:].astype(F32) * edge_scale,
        gains[0] * edge_scale,
        node_total[: 2 * lat].astype(F32) * node_scale,
        node_total[2 * lat :].astype(F32) * node_scale,
        gains[1] * node_scale,
    )


def split_mesh(mesh):
    face, band = mesh.shape["face"], mesh.shape["band"]
    z = 1
    while z * z < face or face % z:
        z += 1
    core = 2 if band % 2 == 0 else 1
    return Mesh(
        mesh.devices.reshape(z, face // z, band // core, core), ("z", "x", "y", "core")
    )


def solution(mesh):
    everyone = ("z", "x", "y", "core")
    rows, split = P(everyone, None), P(everyone)
    return jax.shard_map(
        per_device,
        mesh=split_mesh(mesh),
        in_specs=(
            rows, P(), rows, rows, P(), P(), P(), P(), P(), P(), rows, P(), rows, rows,
            P(everyone, None, None), split, split, split, split,
        ),
        out_specs=(rows, P(), rows, rows, P(), P(), P(), P(), P(), P()),
        check_vma=False,
    )
```

time: 421 us -> 301 us (0.71)
  local copies, waits for them, and re-layouts: 64.5 us -> 11.4 us
  Pallas kernels: 0 us -> 49.1 us
  other arithmetic: 60 us -> 18.9 us
  matrix products: 41.4 us -> 2.72 us
  starting transfers between devices: 18.8 us -> 51 us
  blocking collectives: 105 us -> 77.1 us
  waiting for transfers between devices: 111 us -> 88.3 us
  between operations: 15.2 us -> 0.87 us
    psum x1 -> x0, waiting for transfers between devices: 111 us -> none  [per_device(): lax.psum((node_first_total, node_second_total, node_gain_total, coarse_lo...]
    psum x2 -> x0, blocking collectives: 105 us -> none  [the longest x1 62 us: per_device(): lax.psum(jnp.dot(onehot_rows, new_ups, preferred_element_type=jnp.float32...]
    all_to_all x4 -> x13, waiting for transfers between devices: 0.01 us -> 88.3 us  [the longest x11 72.7 us: swap(): return lax.all_to_all(x, axes, 0, 0, tiled=True)]
    all_to_all x0 -> x10, blocking collectives: none -> 77.1 us  [swap(): return lax.all_to_all(x, axes, 0, 0, tiled=True)]
    pallas_call x0 -> x5, Pallas kernels: none -> 49.1 us  [the longest x1 15.8 us: per_device(): pl.pallas_call(edge_backward_kernel, grid=(steps,), in_specs=[index_spec,...]
    dot_general x26 -> x2, matrix products: 41.4 us -> 2.72 us  [the longest x1 2.5 us: per_device(): lax.dot_general(hot_send, returned, (((0,), (0,)), ((), ())), preferred_e...]
    all_to_all x4 -> x13, starting transfers between devices: 18.6 us -> 51 us  [the longest x11 41.9 us: swap(): return lax.all_to_all(x, axes, 0, 0, tiled=True)]
    gather x11 -> x0, local copies, waits for them, and re-layouts: 27.8 us -> none  [the longest x2 8.03 us: per_device(): jnp.take(fine_grad, edge_receiver, axis=0)]
  transfers between devices with their start and end apart: 5 -> 13, of which waited for: 1 -> 11; matrix products, arithmetic and copies ran while one was open for 18% -> 7% of each run, Pallas kernels for 0% -> 10%
where the time goes in v1:
time: 301 us; the launch traced here: 299 us
  waiting for transfers between devices  88.3 us (29%)
  blocking collectives  77.1 us (26%)
  starting transfers between devices  51 us (17%)
  Pallas kernels  49.1 us (16%)
  other arithmetic  18.9 us (6%)
  local copies, waits for them, and re-layouts  11.4 us (4%)
    all_to_all x10, blocking collectives, swap(): return lax.all_to_all(x, axes, 0, 0, tiled=True)  77.1 us
    all_to_all x11, waiting for transfers between devices, swap(): return lax.all_to_all(x, axes, 0, 0, tiled=True)  72.7 us
    all_to_all x11, starting transfers between devices, swap(): return lax.all_to_all(x, axes, 0, 0, tiled=True)  41.9 us
    pallas_call x1, Pallas kernels, per_device(): pl.pallas_call(edge_backward_kernel, grid=(steps,), in_specs=[index_spec,...  15.8 us
    pallas_call x1, Pallas kernels, per_device(): pl.pallas_call(edge_forward_kernel, grid=(steps,), in_specs=[index_spec,...  14 us
    reduce_sum x9, other arithmetic, reduce_scatter(): x = jnp.sum(got.reshape(count, -1, x.shape[1]).astype(F32), axis=0)  9.98 us
    pallas_call x1, Pallas kernels, per_device(): pl.pallas_call(up_backward_kernel, in_specs=[pl.BlockSpec(memory_space=pl...  9.11 us
    all_to_all x1, waiting for transfers between devices, per_device(): lax.all_to_all(returning.reshape(devices, slots, lat), everyone, 0, 0, ti...  8.18 us
  transfers between devices with their start and end apart: 13, of which 11 were waited for; matrix products, arithmetic and copies ran while one was open for 7% of the time, Pallas kernels for 10%

profile of v1, /device:TPU:0, one launch (start us, length us, event | category | flops | bytes accessed | tf_op | source)
XLA Modules:
  0.0 299.3 jit_solution(5711774141093677961)
XLA Ops:
  5.5 5.8 %all_to_all.171 = bf16[2,512,512]{2,1,0:T(8,128)(2,1)S(1)} all-to-all(bf16[2,512,512]{2,1,0:T(8,128)(2,1)} %bitcast.44), channel_id=1, replica_groups=mesh['z'=4,'x'=2,'y'=2,'core'=2] {'core'}, dimensions={0} | all-to-all | bytes 2097152 | tf_op jit(solution)/shard_map/all_to_all | solution.py:235
  12.5 5.2 %all-to-all-start.2 = ((bf16[4,128,512]{2,1,0:T(8,128)(2,1)}), bf16[4,128,512]{2,1,0:T(8,128)(2,1)S(1)}, u32[]{:S(2)}, u32[]{:S(2)}) async-start(bf16[4,128,512]{2,1,0:T(8,128)(2,1)} %bitcast.8), calls=%async_computation.2 | async-start | bytes 1048576 | tf_op jit(solution)/shard_map/all_to_all | solution.py:235
  18.8 7.2 %all-to-all-done.2 = bf16[4,128,512]{2,1,0:T(8,128)(2,1)S(1)} async-done(((bf16[4,128,512]{2,1,0:T(8,128)(2,1)}), bf16[4,128,512]{2,1,0:T(8,128)(2,1)S(1)}, u32[]{:S(2)}, u32[]{:S(2)}) %all-to-all-start.2) | async-done | bytes 524320 | tf_op jit(solution)/shard_map/all_to_all | solution.py:235
  26.0 4.9 %all-to-all-start = ((bf16[32,4,512]{2,1,0:T(4,128)(2,1)}), bf16[32,4,512]{2,1,0:T(4,128)(2,1)S(1)}, u32[]{:S(2)}, u32[]{:S(2)}) async-start(bf16[32,4,512]{2,1,0:T(4,128)(2,1)} %reshape.168), calls=%async_computation | async-start | bytes 262144 | tf_op jit(solution)/shard_map/all_to_all | solution.py:305
  31.6 7.4 %all-to-all-done = bf16[32,4,512]{2,1,0:T(4,128)(2,1)S(1)} async-done(((bf16[32,4,512]{2,1,0:T(4,128)(2,1)}), bf16[32,4,512]{2,1,0:T(4,128)(2,1)S(1)}, u32[]{:S(2)}, u32[]{:S(2)}) %all-to-all-start) | async-done | bytes 131104 | tf_op jit(solution)/shard_map/all_to_all | solution.py:305
  45.1 14.0 %edge_forward.1 = (f32[1024,512]{1,0:T(8,128)}, bf16[1024,512]{1,0:T(8,128)(2,1)}, f32[256,512]{1,0:T(8,128)}, f32[256,512]{1,0:T(8,128)}, f32[1024,512]{1,0:T(8...) custom-call(s32[1,1024]{1,0:T(1,128)} %bitcast.51, s32[1,1024]{1,0:T(1,128)} %bitcast.53, bf16[1024,512]{1,0:T(8,128)(2,1)} %edge.3, ...), custom_call_target="tpu_custom_call" | custom-call | tf_op jit(solution)/shard_map/edge_forward/pallas_call | solution.py:326
  59.7 5.3 %coarse_mlp.1 = (bf16[32,512]{1,0:T(8,128)(2,1)}, f32[32,512]{1,0:T(8,128)}, bf16[1536,512]{1,0:T(8,128)(2,1)}, f32[1,512]{1,0:T(1,128)}) custom-call(bf16[32,512]{1,0:T(8,128)(2,1)} %constant_dynamic-slice_fusion.1.rows, f32[32,512]{1,0:T(8,128)} %convert_reduce_fusion.total_in, bf16[32,512]{1,0:T(8,128)(2,1)} %constant_dynamic-slice_fusion.ccot, ...), custom_call_target="tpu_custom_call" | custom-call | tf_op jit(solution)/shard_map/coarse_mlp/pallas_call | solution.py:378
  65.8 10.9 %all_to_all.172 = bf16[4,32,512]{2,1,0:T(8,128)(2,1)S(1)} all-to-all(bf16[4,32,512]{2,1,0:T(8,128)(2,1)S(1)} %broadcast_in_dim.36), channel_id=1, replica_groups=mesh['z'=4,'x'=2,'y'=2,'core'=2] {'z'}, dimensions={0} | all-to-all | bytes 262144 | tf_op jit(solution)/shard_map/all_to_all | solution.py:235
  81.1 15.8 %edge_backward.1 = (f32[1024,512]{1,0:T(8,128)}, f32[1536,512]{1,0:T(8,128)}, f32[512,512]{1,0:T(8,128)}, f32[1,512]{1,0:T(1,128)}, f32[256,512]{1,0:T(8,128)}, ...) custom-call(s32[1,1024]{1,0:T(1,128)} %bitcast.52, s32[1,1024]{1,0:T(1,128)} %bitcast.54, bf16[1024,512]{1,0:T(8,128)(2,1)} %edge.3, ...), custom_call_target="tpu_custom_call" | custom-call | tf_op jit(solution)/shard_map/edge_backward/pallas_call | solution.py:345
  98.6 5.4 %all_to_all.173 = bf16[2,512,512]{2,1,0:T(8,128)(2,1)} all-to-all(bf16[2,512,512]{2,1,0:T(8,128)(2,1)S(1)} %broadcast_in_dim.40), channel_id=1, replica_groups=mesh['z'=4,'x'=2,'y'=2,'core'=2] {'core'}, dimensions={0} | all-to-all | bytes 2097152 | tf_op jit(solution)/shard_map/all_to_all | solution.py:235
  103.9 9.1 %up_backward.1 = (f32[256,512]{1,0:T(8,128)}, f32[256,512]{1,0:T(8,128)}, bf16[3072,512]{1,0:T(8,128)(2,1)}, f32[1,512]{1,0:T(1,128)}) custom-call(s32[1,256]{1,0:T(1,128)} %bitcast.58, s32[1,256]{1,0:T(1,128)} %bitcast.60, s32[1]{0:T(128)} %bitcast.6.own, bf16[256,512]{1,0:T(8,128)(2,1)} %up.3, bf16[256,512]{1,0:T(8,128)(2,1)} %get-tuple-element.41.xs, ...), custom_call_target="tpu_custom_call" | custom-call | tf_op jit(solution)/shard_map/up_backward/pallas_call | solution.py:391
  121.7 8.2 %all-to-all-done.7 = bf16[32,4,512]{2,1,0:T(4,128)(2,1)S(1)} async-done(((bf16[32,4,512]{2,1,0:T(4,128)(2,1)}), bf16[32,4,512]{2,1,0:T(4,128)(2,1)S(1)}, u32[]{:S(2)}, u32[]{:S(2)}) %all-to-all-start.7) | async-done | bytes 131104 | tf_op jit(solution)/shard_map/all_to_all | solution.py:369
  129.9 6.1 %all_to_all.175 = bf16[2,768,512]{2,1,0:T(8,128)(2,1)} all-to-all(bf16[2,768,512]{2,1,0:T(8,128)(2,1)S(1)} %bitcast.41), channel_id=1, replica_groups=mesh['z'=4,'x'=2,'y'=2,'core'=2] {'core'}, dimensions={0} | all-to-all | bytes 3145728 | tf_op jit(solution)/shard_map/all_to_all | solution.py:235
  136.0 6.2 %all_to_all.176 = bf16[2,1536,512]{2,1,0:T(8,128)(2,1)S(1)} all-to-all(bf16[2,1536,512]{2,1,0:T(8,128)(2,1)S(1)} %bitcast.38), channel_id=1, replica_groups=mesh['z'=4,'x'=2,'y'=2,'core'=2] {'core'}, dimensions={0} | all-to-all | bytes 6291456 | tf_op jit(solution)/shard_map/all_to_all | solution.py:235
  155.0 10.3 %all-to-all-done.18 = bf16[4,192,512]{2,1,0:T(8,128)(2,1)} async-done(((bf16[4,192,512]{2,1,0:T(8,128)(2,1)}), bf16[4,192,512]{2,1,0:T(8,128)(2,1)}, u32[]{:S(2)}, u32[]{:S(2)}) %all-to-all-start.18) | async-done | bytes 786464 | tf_op jit(solution)/shard_map/all_to_all | solution.py:235
  188.0 17.1 %all-to-all-done.9 = bf16[4,384,512]{2,1,0:T(8,128)(2,1)S(1)} async-done(((bf16[4,384,512]{2,1,0:T(8,128)(2,1)}), bf16[4,384,512]{2,1,0:T(8,128)(2,1)S(1)}, u32[]{:S(2)}, u32[]{:S(2)}) %all-to-all-start.9) | async-done | bytes 1572896 | tf_op jit(solution)/shard_map/all_to_all | solution.py:235
  209.7 5.8 %all-to-all-done.20 = bf16[4,48,512]{2,1,0:T(8,128)(2,1)S(1)} async-done(((bf16[4,48,512]{2,1,0:T(8,128)(2,1)}), bf16[4,48,512]{2,1,0:T(8,128)(2,1)S(1)}, u32[]{:S(2)}, u32[]{:S(2)}) %all-to-all-start.20) | async-done | bytes 196640 | tf_op jit(solution)/shard_map/all_to_all | solution.py:235
  215.5 11.9 %all_to_all.177 = bf16[4,96,512]{2,1,0:T(8,128)(2,1)S(1)} all-to-all(bf16[4,96,512]{2,1,0:T(8,128)(2,1)S(1)} %bitcast.42), channel_id=1, replica_groups=mesh['z'=4,'x'=2,'y'=2,'core'=2] {'z'}, dimensions={0} | all-to-all | bytes 786432 | tf_op jit(solution)/shard_map/all_to_all | solution.py:235
  228.4 5.2 %all-to-all-start.21 = ((bf16[4,192,512]{2,1,0:T(8,128)(2,1)}), bf16[4,192,512]{2,1,0:T(8,128)(2,1)S(1)}, u32[]{:S(2)}, u32[]{:S(2)}) async-start(bf16[4,192,512]{2,1,0:T(8,128)(2,1)} %broadcast_in_dim.100), calls=%async_computation.21 | async-start | bytes 1572864 | tf_op jit(solution)/shard_map/all_to_all | solution.py:235
  233.6 9.9 %all-to-all-done.21 = bf16[4,192,512]{2,1,0:T(8,128)(2,1)S(1)} async-done(((bf16[4,192,512]{2,1,0:T(8,128)(2,1)}), bf16[4,192,512]{2,1,0:T(8,128)(2,1)S(1)}, u32[]{:S(2)}, u32[]{:S(2)}) %all-to-all-start.21) | async-done | bytes 786464 | tf_op jit(solution)/shard_map/all_to_all | solution.py:235
  243.6 5.0 %all_to_all.178 = bf16[2,768,512]{2,1,0:T(8,128)(2,1)S(1)} all-to-all(bf16[2,768,512]{2,1,0:T(8,128)(2,1)S(1)} %broadcast_in_dim.102), channel_id=1, replica_groups=mesh['z'=4,'x'=2,'y'=2,'core'=2] {'core'}, dimensions={0} | all-to-all | bytes 3145728 | tf_op jit(solution)/shard_map/all_to_all | solution.py:235
  248.7 15.7 %all_to_all.179 = bf16[4,96,512]{2,1,0:T(8,128)(2,1)S(1)} all-to-all(bf16[4,96,512]{2,1,0:T(8,128)(2,1)S(1)} %broadcast_in_dim.41), channel_id=1, replica_groups=mesh['z'=4,'x'=2,'y'=2,'core'=2] {'z'}, dimensions={0} | all-to-all | bytes 786432 | tf_op jit(solution)/shard_map/all_to_all | solution.py:235
  275.1 12.9 %all-to-all-done.12 = bf16[4,384,512]{2,1,0:T(8,128)(2,1)S(1)} async-done(((bf16[4,384,512]{2,1,0:T(8,128)(2,1)}), bf16[4,384,512]{2,1,0:T(8,128)(2,1)S(1)}, u32[]{:S(2)}, u32[]{:S(2)}) %all-to-all-start.12) | async-done | bytes 1572896 | tf_op jit(solution)/shard_map/all_to_all | solution.py:235
  288.2 6.3 %all_to_all.180 = bf16[2,1536,512]{2,1,0:T(8,128)(2,1)S(1)} all-to-all(bf16[2,1536,512]{2,1,0:T(8,128)(2,1)S(1)} %broadcast_in_dim.45), channel_id=1, replica_groups=mesh['z'=4,'x'=2,'y'=2,'core'=2] {'core'}, dimensions={0} | all-to-all | bytes 6291456 | tf_op jit(solution)/shard_map/all_to_all | solution.py:235
  (72 shorter events, 86.8 us)
Async XLA Ops:
  0.6 43.1 %copy-start = (bf16[1024,512]{1,0:T(8,128)(2,1)S(1)}, bf16[1024,512]{1,0:T(8,128)(2,1)}, u32[]{:S(2)}) copy-start(bf16[1024,512]{1,0:T(8,128)(2,1)} %param.30) | copy-start | bytes 3145732
  5.5 12.1 %copy-start.5 = (s32[1,32,4]{1,2,0:T(4,128)S(1)}, s32[1,32,4]{1,2,0:T(4,128)}, u32[]{:S(2)}) copy-start(s32[1,32,4]{1,2,0:T(4,128)} %param.33) | copy-start | bytes 1540
  5.5 12.3 %copy-start.2 = (bf16[256,512]{1,0:T(8,128)(2,1)S(1)}, bf16[256,512]{1,0:T(8,128)(2,1)}, u32[]{:S(2)}) copy-start(bf16[256,512]{1,0:T(8,128)(2,1)} %node.5) | copy-start | bytes 786436
  12.5 13.5 %all-to-all-start.2 = ((bf16[4,128,512]{2,1,0:T(8,128)(2,1)}), bf16[4,128,512]{2,1,0:T(8,128)(2,1)S(1)}, u32[]{:S(2)}, u32[]{:S(2)}) async-start(bf16[4,128,512]{2,1,0:T(8,128)(2,1)} %bitcast.8), calls=%async_computation.2 | async-start | bytes 1048576 | tf_op jit(solution)/shard_map/all_to_all | solution.py:235
  26.0 13.1 %all-to-all-start = ((bf16[32,4,512]{2,1,0:T(4,128)(2,1)}), bf16[32,4,512]{2,1,0:T(4,128)(2,1)S(1)}, u32[]{:S(2)}, u32[]{:S(2)}) async-start(bf16[32,4,512]{2,1,0:T(4,128)(2,1)} %reshape.168), calls=%async_computation | async-start | bytes 262144 | tf_op jit(solution)/shard_map/all_to_all | solution.py:305
  39.0 20.0 %all-to-all-start.3 = ((bf16[4,32,512]{2,1,0:T(8,128)(2,1)}), bf16[4,32,512]{2,1,0:T(8,128)(2,1)S(1)}, u32[]{:S(2)}, u32[]{:S(2)}) async-start(bf16[4,32,512]{2,1,0:T(8,128)(2,1)} %bitcast.9), calls=%async_computation.3 | async-start | bytes 262144 | tf_op jit(solution)/shard_map/all_to_all | solution.py:235
  77.6 20.9 %all-to-all-start.5 = ((bf16[4,128,512]{2,1,0:T(8,128)(2,1)}), bf16[4,128,512]{2,1,0:T(8,128)(2,1)S(1)}, u32[]{:S(2)}, u32[]{:S(2)}) async-start(bf16[4,128,512]{2,1,0:T(8,128)(2,1)} %broadcast_in_dim.38), calls=%async_computation.5 | async-start | bytes 1048576 | tf_op jit(solution)/shard_map/all_to_all | solution.py:235
  103.9 9.1 %copy-start.6 = (f32[1,512]{1,0:T(1,128)S(1)}, f32[1,512]{1,0:T(1,128)}, u32[]{:S(2)}) copy-start(f32[1,512]{1,0:T(1,128)} %get-tuple-element.60) | copy-start | bytes 6148
  103.9 26.0 %copy-start.4 = (bf16[1536,512]{1,0:T(8,128)(2,1)S(1)}, bf16[1536,512]{1,0:T(8,128)(2,1)}, u32[]{:S(2)}) copy-start(bf16[1536,512]{1,0:T(8,128)(2,1)} %get-tuple-element.61) | copy-start | bytes 4718596
  117.5 12.4 %all-to-all-start.7 = ((bf16[32,4,512]{2,1,0:T(4,128)(2,1)}), bf16[32,4,512]{2,1,0:T(4,128)(2,1)S(1)}, u32[]{:S(2)}, u32[]{:S(2)}) async-start(bf16[32,4,512]{2,1,0:T(4,128)(2,1)} %reshape.175), calls=%async_computation.7 | async-start | bytes 262144 | tf_op jit(solution)/shard_map/all_to_all | solution.py:369
  129.9 6.1 %copy-start.3 = (bf16[3072,512]{1,0:T(8,128)(2,1)S(1)}, bf16[3072,512]{1,0:T(8,128)(2,1)}, u32[]{:S(2)}) copy-start(bf16[3072,512]{1,0:T(8,128)(2,1)} %get-tuple-element.56) | copy-start | bytes 9437188
  142.8 7.9 %all-to-all-start.15 = ((f32[4,2,512]{2,1,0:T(2,128)}), f32[4,2,512]{2,1,0:T(2,128)S(1)}, u32[]{:S(2)}, u32[]{:S(2)}) async-start(f32[4,2,512]{2,1,0:T(2,128)} %broadcast_in_dim.47), calls=%async_computation.15 | async-start | bytes 32768 | tf_op jit(solution)/shard_map/all_to_all | solution.py:235
  150.8 14.5 %all-to-all-start.18 = ((bf16[4,192,512]{2,1,0:T(8,128)(2,1)}), bf16[4,192,512]{2,1,0:T(8,128)(2,1)}, u32[]{:S(2)}, u32[]{:S(2)}) async-start(bf16[4,192,512]{2,1,0:T(8,128)(2,1)} %bitcast.37), calls=%async_computation.18 | async-start | bytes 1572864 | tf_op jit(solution)/shard_map/all_to_all | solution.py:235
  165.9 8.8 %all-to-all-start.16 = ((f32[4,2,512]{2,1,0:T(2,128)}), f32[4,2,512]{2,1,0:T(2,128)S(1)}, u32[]{:S(2)}, u32[]{:S(2)}) async-start(f32[4,2,512]{2,1,0:T(2,128)} %broadcast_in_dim.48), calls=%async_computation.16 | async-start | bytes 32768 | tf_op jit(solution)/shard_map/all_to_all | solution.py:235
  174.8 9.6 %all-to-all-start.19 = ((bf16[4,48,512]{2,1,0:T(8,128)(2,1)}), bf16[4,48,512]{2,1,0:T(8,128)(2,1)S(1)}, u32[]{:S(2)}, u32[]{:S(2)}) async-start(bf16[4,48,512]{2,1,0:T(8,128)(2,1)} %bitcast.22), calls=%async_computation.19 | async-start | bytes 393216 | tf_op jit(solution)/shard_map/all_to_all | solution.py:235
  184.3 20.7 %all-to-all-start.9 = ((bf16[4,384,512]{2,1,0:T(8,128)(2,1)}), bf16[4,384,512]{2,1,0:T(8,128)(2,1)S(1)}, u32[]{:S(2)}, u32[]{:S(2)}) async-start(bf16[4,384,512]{2,1,0:T(8,128)(2,1)} %bitcast.34), calls=%async_computation.9 | async-start | bytes 3145728 | tf_op jit(solution)/shard_map/all_to_all | solution.py:235
  205.7 9.8 %all-to-all-start.20 = ((bf16[4,48,512]{2,1,0:T(8,128)(2,1)}), bf16[4,48,512]{2,1,0:T(8,128)(2,1)S(1)}, u32[]{:S(2)}, u32[]{:S(2)}) async-start(bf16[4,48,512]{2,1,0:T(8,128)(2,1)} %broadcast_in_dim.98), calls=%async_computation.20 | async-start | bytes 393216 | tf_op jit(solution)/shard_map/all_to_all | solution.py:235
  228.4 15.2 %all-to-all-start.21 = ((bf16[4,192,512]{2,1,0:T(8,128)(2,1)}), bf16[4,192,512]{2,1,0:T(8,128)(2,1)S(1)}, u32[]{:S(2)}, u32[]{:S(2)}) async-start(bf16[4,192,512]{2,1,0:T(8,128)(2,1)} %broadcast_in_dim.100), calls=%async_computation.21 | async-start | bytes 1572864 | tf_op jit(solution)/shard_map/all_to_all | solution.py:235
  265.6 22.4 %all-to-all-start.12 = ((bf16[4,384,512]{2,1,0:T(8,128)(2,1)}), bf16[4,384,512]{2,1,0:T(8,128)(2,1)S(1)}, u32[]{:S(2)}, u32[]{:S(2)}) async-start(bf16[4,384,512]{2,1,0:T(8,128)(2,1)} %broadcast_in_dim.43), calls=%async_computation.12 | async-start | bytes 3145728 | tf_op jit(solution)/shard_map/all_to_all | solution.py:235
  294.5 4.9 %copy-start.1 = (bf16[1024,512]{1,0:T(8,128)(2,1)S(1)}, bf16[1024,512]{1,0:T(8,128)(2,1)}, u32[]{:S(2)}) copy-start(bf16[1024,512]{1,0:T(8,128)(2,1)} %param.30) | copy-start | bytes 3145732
